TPU v7x, 32 devices: a whole 2x2x4 slice. The times are simulated.
32 devices in a mesh: section: 4 (over y, x), student: 2 (over core), dp: 4 (over z).
Axes of the slice: x: 2, y: 2, z: 4, core: 2. Of those that a mesh axis runs over, the one named last changes fastest.
Arguments:
- in_flight: bfloat16 [4, 2, 128, 4096], P('section', 'student'), may hold values from -6 to 6
- segments: int32 [4, 2, 128], P(None, 'student'), may hold values from 0 to 3, never falling along the last dimension, each value on 1 to 64 neighbouring positions
- norm_gain: float32 [4, 4096], P('section'), may hold values from 0.5 to 1.5
- w_qkv: bfloat16 [4, 4096, 3, 1024], P('section', None, None, 'dp')
- w_out: bfloat16 [4, 1024, 4096], P('section', 'dp'), may hold values from -0.1875 to 0.1875
- final_gain: float32 [4096], replicated, may hold values from 0.25 to 1.75
- student_rows: bfloat16 [2, 3, 2, 128, 1024], P('student', None, None, 'dp'), may hold values from -6 to 6
- student_gain: float32 [2, 1024], P('student'), may hold values from 0.5 to 1.5
- w_head: bfloat16 [2, 1024, 4096], P('student', None, 'section'), may hold values from -0.1875 to 0.1875
Outputs:
- advanced: bfloat16 [4, 2, 128, 4096], P('section', 'student', 'dp')
- grad_head: float32 [2, 1024, 4096], P('student', 'dp', 'section')
Inputs may be any that keep to these rules, and one draw needn't show every extreme that they name: `segments`: along a micro-batch's tokens the crop numbers never fall; each of the 4 crops holds 1 to 64 tokens and one holds exactly 64.
All inputs are finite; a program needn't handle non-finite values.
Results may differ from a plain program's by a relative error of at most 0.025.
Values may be sent and summed in bfloat16 or wider, within the bound.
A program may use at most 64 MiB of HBM per device.

v0:
```python
import functools

import jax
import jax.numpy as jnp
from jax import lax
from jax.experimental import pallas as pl
from jax.experimental.pallas import tpu as pltpu
from jax.sharding import PartitionSpec as P

HEAD_SIZE = 128
LN_ROWS = 16
BF16 = jnp.bfloat16
F32 = jnp.float32
MESH = pl.DeviceIdType.MESH


def layer_norm(rows, gain):
    rows = rows.astype(F32)
    centred = rows - jnp.mean(rows, axis=-1, keepdims=True)
    spread = jnp.mean(centred * centred, axis=-1, keepdims=True)
    return centred * lax.rsqrt(spread + 1e-06) * gain


def attend(query, keys, values, same):
    scores = lax.dot_general(
        query, keys, (((1,), (1,)), ((), ())), preferred_element_type=F32
    ) * HEAD_SIZE ** (-0.5)
    scores = jnp.where(same, scores, -1e30)
    top = jnp.max(scores, axis=-1, keepdims=True)
    expo = jnp.exp(scores - top)
    probs = (expo / jnp.sum(expo, axis=-1, keepdims=True)).astype(BF16)
    return jnp.dot(probs, values, preferred_element_type=F32).astype(BF16)


def window_kernel(
    S, M, Z, T, R,
    x_ref, seg_ref, gain_ref, wqkv_ref, wout_ref, fgain_ref, srows_ref, sgain_ref, whead_ref,
    adv_ref, grad_ref,
    wqkv, wofull, whead, normed, xfull, mixfull, xs, xrows, fin, tg, tbuf, advbuf,
    sall, pred, fown, errs,
    local_sem, wo_s, wo_r, wf_s, wf_r, mx_s, mx_r, sh_s, sh_r, ar_s, ar_r, al_s, al_r,
    ro_s, ro_r, ad_s, ad_r, tg_s, tg_r, fe_s, fe_r, fp_s, fp_r,
    er_s, er_r, ml_s, ml_r,
):
    s = lax.axis_index("section")
    c = lax.axis_index("student")
    z = lax.axis_index("dp")
    root = S - 1
    tokens, model = x_ref.shape
    wid = wout_ref.shape[0]
    share = tokens // Z
    cw = model // Z
    block = whead_ref.shape[1]
    sw = whead_ref.shape[0]
    fw = sw // Z
    ow = sw // S
    step_rows = tokens // R
    halves = 2 if M % 2 == 0 else 1
    part = c % halves
    hw = wid // halves
    sends = []

    def remote(src, dst, send, recv, where):
        return pltpu.make_async_remote_copy(
            src_ref=src, dst_ref=dst, send_sem=send, recv_sem=recv,
            device_id=where, device_id_type=MESH,
        )

    def post(cond, build):
        if cond is True:
            build().start()
        else:
            pl.when(cond)(lambda: build().start())
        sends.append((cond, build))

    def zmod(value):
        return lax.rem(value + Z, Z)

    def cols(index):
        return pl.ds(pl.multiple_of(index * cw, 128), cw)

    load_qkv = pltpu.make_async_copy(wqkv_ref, wqkv, local_sem.at[0])
    load_head = pltpu.make_async_copy(whead_ref, whead, local_sem.at[1])
    own_wo = pltpu.make_async_copy(
        wout_ref.at[:, cols(z)],
        wofull.at[pl.ds(pl.multiple_of(z * wid, wid), wid), :],
        local_sem.at[2],
    )
    load_qkv.start()
    own_wo.start()
    load_head.start()

    barrier = pltpu.get_barrier_semaphore()

    def greet(where):
        pl.semaphore_signal(barrier, inc=1, device_id=where, device_id_type=MESH)

    for k in range(1, Z):
        greet((s, c, zmod(z + k)))
    for k in range(Z):
        pl.when(s > 0)(functools.partial(greet, (s - 1, c, zmod(z + k))))
        pl.when(s < root)(functools.partial(greet, (s + 1, c, zmod(z + k))))
    for at in range(S):
        far = jnp.logical_or(s - at > 1, at - s > 1)
        pl.when(far)(functools.partial(greet, (jnp.int32(at), c, z)))
        for dm in range(1, M):
            greet((jnp.int32(at), lax.rem(c + dm, M), z))
    for at in range(S):
        near = min(at, 1) + min(root - at, 1)
        peers = (Z - 1) + Z * near + (S - 1 - near) + S * (M - 1)
        pl.when(s == at)(functools.partial(pl.semaphore_wait, barrier, peers))

    def wo_rows(source, which):
        return pl.ds(pl.multiple_of(source * wid + which * hw, hw), hw)

    for k in sorted(range(1, Z), reverse=True):
        def build(k=k):
            to = zmod(z + k)
            return remote(
                wout_ref.at[pl.ds(pl.multiple_of(part * hw, hw), hw), cols(to)],
                wofull.at[wo_rows(z, part), :],
                wo_s.at[k - 1], wo_r.at[k - 1], (s, c, to),
            )
        post(True, build)

    def pass_on(k):
        source = zmod(z - k)
        mine = wofull.at[wo_rows(source, part), :]
        mate = c + 1 - 2 * part
        return remote(mine, mine, wf_s.at[k - 1], wf_r.at[k - 1], (s, mate, z))

    def gather_wo():
        for k in range(1, Z):
            source = zmod(z - k)
            mine = wofull.at[wo_rows(source, part), :]
            remote(mine, mine, wo_s.at[k - 1], wo_r.at[k - 1], (s, c, source)).wait_recv()
            if halves == 2:
                post(True, functools.partial(pass_on, k))
        if halves == 2:
            for k in range(1, Z):
                source = zmod(z - k)
                other = wofull.at[wo_rows(source, 1 - part), :]
                remote(other, other, wf_s.at[k - 1], wf_r.at[k - 1],
                       (s, c + 1 - 2 * part, z)).wait_recv()
        own_wo.wait()

    def scols(index):
        return pl.ds(pl.multiple_of(index * ow, 128), ow)

    def spread_rows():
        sall[0] = srows_ref[...]
        for k in range(1, Z):
            def build(k=k):
                return remote(srows_ref.at[:, :, :, scols(s)], sall.at[k, :, :, :, scols(s)],
                              fe_s.at[k - 1], fe_r.at[k - 1], (s, c, zmod(z + k)))
            post(True, build)

    def pass_rows():
        for k in range(1, Z):
            there = sall.at[k, :, :, :, scols(s)]
            remote(there, there, fe_s.at[k - 1], fe_r.at[k - 1], (s, c, zmod(z - k))).wait_recv()
        for k in range(1, S):
            def build(k=k):
                there = sall.at[pl.ds(1, Z - 1), :, :, :, scols(s)]
                return remote(there, there, fp_s.at[k - 1], fp_r.at[k - 1],
                              (lax.rem(s + k, S), c, z))
            post(True, build)

    def student():
        for k in range(1, S):
            where = lax.rem(s + S - k, S)
            there = sall.at[pl.ds(1, Z - 1), :, :, :, scols(where)]
            remote(there, there, fp_s.at[k - 1], fp_r.at[k - 1], (where, c, z)).wait_recv()
        load_head.wait()

        def one(k, carry):
            rows = layer_norm(sall[k].astype(F32).reshape(T * M * share, sw), sgain_ref[...])
            rows = rows.astype(BF16)
            for zz in range(Z):
                def own(zz=zz):
                    fown[k] = rows[:, zz * fw:(zz + 1) * fw].reshape(T, M * share, fw)
                pl.when(z == zz)(own)
            pred[k] = jnp.dot(rows, whead[...], preferred_element_type=F32).reshape(
                T, M, share, block
            )
            return carry

        lax.fori_loop(0, Z, one, 0)

    def spread(t):
        def take():
            there = tbuf.at[t, c, 0]
            remote(there, there, tg_s.at[t, 0], tg_r.at[t], (root, c, z)).wait_recv()
        pl.when(s != root)(take)
        for k in range(1, Z):
            def build(k=k):
                return remote(tbuf.at[t, c, 0], tbuf.at[t, c, k], er_s.at[t, k - 1],
                              er_r.at[t, k - 1], (s, c, zmod(z + k)))
            post(True, build)

    def relay(t):
        for k in range(Z):
            there = tbuf.at[t, c, k]
            if k:
                remote(there, there, er_s.at[t, k - 1], er_r.at[t, k - 1],
                       (s, c, zmod(z - k))).wait_recv()
            for dm in range(1, M):
                def build(k=k, dm=dm):
                    there = tbuf.at[t, c, k]
                    return remote(there, there, ml_s.at[t, dm - 1, k], ml_r.at[t, dm - 1, k],
                                  (s, lax.rem(c + dm, M), z))
                post(True, build)

    def gradient(t):
        for dm in range(1, M):
            for k in range(Z):
                who = lax.rem(c + M - dm, M)
                there = tbuf.at[t, who, k]
                remote(there, there, ml_s.at[t, dm - 1, k], ml_r.at[t, dm - 1, k],
                       (s, who, z)).wait_recv()

        def one(k, carry):
            err = (pred[k, t] - tbuf[t, :, k].astype(F32)) * (2.0 / tokens)
            errs[k] = err.reshape(M * share, block).astype(BF16)
            return carry

        lax.fori_loop(0, Z, one, 0)
        term = lax.dot_general(
            fown[:, t].reshape(Z * M * share, fw), errs[...].reshape(Z * M * share, block),
            (((0,), (0,)), ((), ())), preferred_element_type=F32,
        )
        if t == 0:
            grad_ref[...] = term
        else:
            grad_ref[...] += term

    def gather_state(t, active):
        def piece(r, origin):
            return xfull.at[t - 1, pl.ds(r * step_rows, step_rows), cols(origin)]

        def to_right(r, k):
            there = piece(r, z - k)
            return remote(there, there, ar_s.at[t - 1, k, r], ar_r.at[t - 1, k, r], (s, c, z + 1))

        def to_left(r, k):
            there = piece(r, z + k)
            return remote(there, there, al_s.at[t - 1, k, r], al_r.at[t - 1, k, r], (s, c, z - 1))

        def right_from(r, k):
            there = piece(r, z - k)
            remote(there, there, ar_s.at[t - 1, k - 1, r], ar_r.at[t - 1, k - 1, r],
                   (s, c, z - 1)).wait_recv()

        def left_from(r, k):
            there = piece(r, z + k)
            remote(there, there, al_s.at[t - 1, k - 1, r], al_r.at[t - 1, k - 1, r],
                   (s, c, z + 1)).wait_recv()

        for r in range(R):
            def first(r=r):
                there = piece(r, z)
                remote(there, there, sh_s.at[t - 1, r], sh_r.at[t - 1, r],
                       (s - 1, c, z)).wait_recv()
            pl.when(active)(first)
            post(jnp.logical_and(active, z < Z - 1), functools.partial(to_right, r, 0))
            post(jnp.logical_and(active, z > 0), functools.partial(to_left, r, 0))
        for k in range(1, Z):
            for r in range(R):
                pl.when(jnp.logical_and(active, z >= k))(functools.partial(right_from, r, k))
                if k < Z - 1:
                    post(jnp.logical_and(active, jnp.logical_and(z >= k, z < Z - 1)),
                         functools.partial(to_right, r, k))
                pl.when(jnp.logical_and(active, z + k < Z))(functools.partial(left_from, r, k))
                if k < Z - 1:
                    post(jnp.logical_and(active, jnp.logical_and(z + k < Z, z > 0)),
                         functools.partial(to_left, r, k))

    def mix_cols(index):
        return pl.ds(pl.multiple_of(index * wid, 128), wid)

    def mixing(t):
        source = x_ref if t == 0 else xfull.at[t - 1]

        def norm_rows(i, carry):
            rows = pl.ds(pl.multiple_of(i * LN_ROWS, LN_ROWS), LN_ROWS)
            normed[rows, :] = layer_norm(source[rows, :], gain_ref[...]).astype(BF16)
            return carry

        lax.fori_loop(0, tokens // LN_ROWS, norm_rows, 0)
        if t == 0:
            load_qkv.wait()
        rows = normed[...]
        query, keys, values = [
            jnp.dot(rows, wqkv[j], preferred_element_type=F32).astype(BF16)
            for j in range(3)
        ]
        crops = jnp.broadcast_to(seg_ref[s - t].astype(F32), (tokens, tokens))
        same = crops == crops.T
        outs = []
        for h in range(wid // HEAD_SIZE):
            at = slice(h * HEAD_SIZE, (h + 1) * HEAD_SIZE)
            outs.append(attend(query[:, at], keys[:, at], values[:, at], same))
        mixfull[t, :, mix_cols(z)] = jnp.concatenate(outs, axis=1)

    def send_mixed(t, active):
        for k in range(1, Z):
            def build(k=k):
                own = mixfull.at[t, :, mix_cols(z)]
                return remote(own, own, mx_s.at[t, k - 1], mx_r.at[t, k - 1],
                              (s, c, zmod(z + k)))
            post(active, build)

    def project(t):
        for k in range(1, Z):
            there = mixfull.at[t, :, mix_cols(zmod(z - k))]
            remote(there, there, mx_s.at[t, k - 1], mx_r.at[t, k - 1],
                   (s, c, zmod(z - k))).wait_recv()
        own = x_ref[:, cols(z)] if t == 0 else xfull[t - 1, :, cols(z)]
        summed = own.astype(F32) + jnp.dot(mixfull[t], wofull[...], preferred_element_type=F32)
        if t < T - 1:
            xs[t] = summed.astype(BF16)
        xrows[t] = summed.reshape(Z, share, cw).astype(BF16)

    def send_state(t, active):
        if t < T - 1:
            for r in range(R):
                def build(r=r):
                    at = pl.ds(r * step_rows, step_rows)
                    return remote(xs.at[t, at, :], xfull.at[t, at, cols(z)],
                                  sh_s.at[t, r], sh_r.at[t, r], (s + 1, c, z))
                post(jnp.logical_and(active, s < root), build)
        else:
            for k in range(Z):
                def build(k=k):
                    to = zmod(z + k)
                    return remote(xrows.at[t, to], advbuf.at[:, cols(z)],
                                  ad_s.at[k], ad_r.at[k], (s + 1, c, to))
                post(jnp.logical_and(active, s < root), build)
        for k in range(1, Z):
            def build_row(k=k):
                to = zmod(z + k)
                return remote(xrows.at[t, to], fin.at[t, :, cols(z)],
                              ro_s.at[t, k - 1], ro_r.at[t, k - 1], (s, c, to))
            post(s == root, build_row)

    def finish(t):
        def rows():
            fin[t, :, cols(z)] = xrows[t, z]
            for k in range(1, Z):
                there = fin.at[t, :, cols(zmod(z - k))]
                remote(there, there, ro_s.at[t, k - 1], ro_r.at[t, k - 1],
                       (s, c, zmod(z - k))).wait_recv()
            tg[t] = layer_norm(fin[t], fgain_ref[...]).astype(BF16)
            tbuf[t, c, 0] = tg[t, :, root * block:(root + 1) * block]

        pl.when(s == root)(rows)
        for to in range(root):
            def build(to=to):
                return remote(tg.at[t, :, to * block:(to + 1) * block], tbuf.at[t, c, 0],
                              tg_s.at[t, to], tg_r.at[t], (jnp.int32(to), c, z))
            post(s == root, build)

    for t in range(T):
        active = True if t == 0 else s >= t
        if t == 0:
            mixing(0)
        else:
            gather_state(t, active)
            if t == 1:
                pass_rows()
            else:
                relay(t - 2)
                spread(t - 1)
            pl.when(active)(functools.partial(mixing, t))
        send_mixed(t, active)
        if t == 0:
            spread_rows()
            gather_wo()
            project(0)
        else:
            if t == 1:
                spread(0)
            if t == T - 1:
                relay(t - 1)
                student()
            pl.when(active)(functools.partial(project, t))
        send_state(t, active)
        if t == T - 1:
            for before in range(t):
                gradient(before)
        finish(t)

    spread(T - 1)
    relay(T - 1)
    gradient(T - 1)

    def arrived():
        for k in range(Z):
            there = advbuf.at[:, cols(zmod(z - k))]
            remote(there, there, ad_s.at[k], ad_r.at[k], (s - 1, c, zmod(z - k))).wait_recv()
        adv_ref[...] = advbuf[...]

    def nothing():
        adv_ref[...] = jnp.zeros_like(adv_ref)

    pl.when(s >= T)(arrived)
    pl.when(s < T)(nothing)
    for cond, build in sends:
        if cond is True:
            build().wait_send()
        else:
            pl.when(cond)(lambda build=build: build().wait_send())


def solution(mesh):
    S, M, Z = mesh.shape["section"], mesh.shape["student"], mesh.shape["dp"]

    def on_device(
        in_flight, segments, norm_gain, w_qkv, w_out, final_gain, student_rows, student_gain, w_head
    ):
        tokens, model = in_flight.shape[2:]
        wid = w_out.shape[1]
        T, share = student_rows.shape[1], tokens // Z
        sw, block = w_head.shape[1:]
        cw, fw = model // Z, sw // Z
        R = 4 if Z <= 4 else 2
        vmem = pl.BlockSpec(memory_space=pltpu.VMEM)
        hbm = pl.BlockSpec(memory_space=pl.ANY)
        dma = pltpu.SemaphoreType.DMA
        K = max(Z - 1, 1)
        adv, grad = pl.pallas_call(
            functools.partial(window_kernel, S, M, Z, T, R),
            out_shape=(
                jax.ShapeDtypeStruct((share, model), BF16),
                jax.ShapeDtypeStruct((fw, block), F32),
            ),
            in_specs=[vmem, vmem, vmem, hbm, hbm, vmem, vmem, vmem, hbm],
            out_specs=(vmem, vmem),
            scratch_shapes=[
                pltpu.VMEM((3, model, wid), BF16),
                pltpu.VMEM((Z * wid, cw), BF16),
                pltpu.VMEM((sw, block), BF16),
                pltpu.VMEM((tokens, model), BF16),
                pltpu.VMEM((T - 1, tokens, model), BF16),
                pltpu.VMEM((T, tokens, Z * wid), BF16),
                pltpu.VMEM((T - 1, tokens, cw), BF16),
                pltpu.VMEM((T, Z, share, cw), BF16),
                pltpu.VMEM((T, share, model), BF16),
                pltpu.VMEM((T, share, model), BF16),
                pltpu.VMEM((T, M, Z, share, block), BF16),
                pltpu.VMEM((share, model), BF16),
                pltpu.VMEM((Z, T, M, share, sw), BF16),
                pltpu.VMEM((Z, T, M, share, block), F32),
                pltpu.VMEM((Z, T, M * share, fw), BF16),
                pltpu.VMEM((Z, M * share, block), BF16),
                dma((3,)),
                dma((K,)), dma((K,)), dma((K,)), dma((K,)),
                dma((T, K)), dma((T, K)),
                dma((T - 1, R)), dma((T - 1, R)),
                dma((T - 1, K, R)), dma((T - 1, K, R)),
                dma((T - 1, K, R)), dma((T - 1, K, R)),
                dma((T, K)), dma((T, K)),
                dma((Z,)), dma((Z,)),
                dma((T, S)), dma((T,)),
                dma((K,)), dma((K,)), dma((S,)), dma((S,)),
                dma((T, K)), dma((T, K)),
                dma((T, M, Z)), dma((T, M, Z)),
            ],
            compiler_params=pltpu.CompilerParams(
                collective_id=0, has_side_effects=True, vmem_limit_bytes=58 << 20
            ),
        )(
            in_flight[0, 0], segments, norm_gain, jnp.transpose(w_qkv[0], (1, 0, 2)), w_out[0],
            final_gain[None], student_rows[0], student_gain, w_head[0],
        )
        return adv[None, None], grad[None]

    in_specs = (
        P("section", "student", None, None),
        P(None, "student", None),
        P("section", None),
        P("section", None, None, "dp"),
        P("section", "dp", None),
        P(),
        P("student", None, None, "dp", None),
        P("student", None),
        P("student", None, "section"),
    )
    out_specs = (P("section", "student", "dp", None), P("student", "dp", "section"))
    return jax.shard_map(
        on_device, mesh=mesh, in_specs=in_specs, out_specs=out_specs, check_vma=False
    )
```

profile of v0, /device:TPU:1, one launch (start us, length us, event | category | flops | bytes accessed | tf_op | source)
XLA Modules:
  0.0 140.1 jit_solution(12333558695064206357)
XLA Ops:
  0.6 135.5 %shard_map.104 = (bf16[32,4096]{1,0:T(8,128)(2,1)}, f32[256,1024]{1,0:T(8,128)}) custom-call(bf16[128,4096]{1,0:T(8,128)(2,1)} %bitcast.13, s32[4,1,128]{2,1,0:T(1,128)} %seg_ref.1, f32[1,4096]{1,0:T(1,128)} %gain_ref.1, bf16[3,4096,256]{2,1,0:T(8,128)(2,1)} %bitcast.10, bf16[256,4096]{1,0:T(8,128)(2,1)} %bitcast.11, f32[1,4096]{1,0:T(1,128)} %bitcast.17, ...), custom_call_target="tpu_custom_call" | custom-call | tf_op jit(solution)/shard_map/pallas_call | solution.py:431
  136.2 1.7 %copy.13 = bf16[1,1,32,4096]{3,2,1,0:T(8,128)(2,1)} copy(bf16[1,1,32,4096]{3,2,1,0:T(8,128)(2,1)} %bitcast.16) | data formatting | bytes 524288
  137.8 2.3 %copy.14 = f32[1,256,1024]{2,1,0:T(8,128)} copy(f32[1,256,1024]{2,1,0:T(8,128)} %bitcast.14) | data formatting | bytes 2097152
where the time goes:
time: 140 us
  Pallas kernels  136 us (97%)
  local copies, waits for them, and re-layouts  3.98 us (3%)
    pallas_call x1, Pallas kernels, on_device(): pl.pallas_call(functools.partial(window_kernel, S, M, Z, T, R), out_shape...  136 us
    unnamed x2, local copies, waits for them, and re-layouts  3.98 us

commit v1 on v0

--- a/solution.py
+++ b/solution.py
@@ -33,14 +33,14 @@
 
 
 def window_kernel(
-    S, M, Z, T, R,
-    x_ref, seg_ref, gain_ref, wqkv_ref, wout_ref, fgain_ref, srows_ref, sgain_ref, whead_ref,
+    S, M, Z, T, pieces, turns,
+    x_hbm, seg_ref, gain_ref, wqkv_ref, wout_ref, fgain_ref, srows_ref, sgain_ref, whead_ref,
     adv_ref, grad_ref,
     wqkv, wofull, whead, normed, xfull, mixfull, xs, xrows, fin, tg, tbuf, advbuf,
-    sall, pred, fown, errs,
-    local_sem, wo_s, wo_r, wf_s, wf_r, mx_s, mx_r, sh_s, sh_r, ar_s, ar_r, al_s, al_r,
+    sall, pred, fown, errs, x_ref, grad, det,
+    local_sem, x_sem, out_sem, wo_s, wo_r, wf_s, wf_r, mx_s, mx_r, sh_s, sh_r, ar_s, ar_r, al_s, al_r,
     ro_s, ro_r, ad_s, ad_r, tg_s, tg_r, fe_s, fe_r, fp_s, fp_r,
-    er_s, er_r, ml_s, ml_r,
+    er_s, er_r, ml_s, ml_r, dz_s, dz_r, dx_s, dx_r,
 ):
     s = lax.axis_index("section")
     c = lax.axis_index("student")
@@ -53,8 +53,11 @@
     block = whead_ref.shape[1]
     sw = whead_ref.shape[0]
     fw = sw // Z
-    ow = sw // S
-    step_rows = tokens // R
+    units = sw // 128
+    other = max(1, units // (2 * S)) * 128
+    first = sw - other * (S - 1)
+    straight = tokens - det.shape[1]
+    turn_rows = det.shape[1] // turns
     halves = 2 if M % 2 == 0 else 1
     part = c % halves
     hw = wid // halves
@@ -86,9 +89,15 @@
         wofull.at[pl.ds(pl.multiple_of(z * wid, wid), wid), :],
         local_sem.at[2],
     )
-    load_qkv.start()
-    own_wo.start()
-    load_head.start()
+    xr = tokens // x_sem.shape[0]
+    load_x = [
+        pltpu.make_async_copy(
+            x_hbm.at[pl.ds(i * xr, xr), :], x_ref.at[pl.ds(i * xr, xr), :], x_sem.at[i]
+        )
+        for i in range(x_sem.shape[0])
+    ]
+    load_rows = pltpu.make_async_copy(srows_ref, sall.at[0], local_sem.at[3])
+    save_adv = pltpu.make_async_copy(advbuf, adv_ref, local_sem.at[4])
 
     barrier = pltpu.get_barrier_semaphore()
 
@@ -105,6 +114,12 @@
         pl.when(far)(functools.partial(greet, (jnp.int32(at), c, z)))
         for dm in range(1, M):
             greet((jnp.int32(at), lax.rem(c + dm, M), z))
+    for copy in load_x:
+        copy.start()
+    load_qkv.start()
+    own_wo.start()
+    load_rows.start()
+    load_head.start()
     for at in range(S):
         near = min(at, 1) + min(root - at, 1)
         peers = (Z - 1) + Z * near + (S - 1 - near) + S * (M - 1)
@@ -144,34 +159,43 @@
                        (s, c + 1 - 2 * part, z)).wait_recv()
         own_wo.wait()
 
-    def scols(index):
-        return pl.ds(pl.multiple_of(index * ow, 128), ow)
-
-    def spread_rows():
-        sall[0] = srows_ref[...]
+    def portion(index, zero):
+        if zero:
+            return pl.ds(0, first)
+        return pl.ds(pl.multiple_of(first + (index - 1) * other, 128), other)
+
+    def spread_rows(zero):
+        cond = s == 0 if zero else s > 0
         for k in range(1, Z):
             def build(k=k):
-                return remote(srows_ref.at[:, :, :, scols(s)], sall.at[k, :, :, :, scols(s)],
+                part = portion(s, zero)
+                return remote(srows_ref.at[:, :, :, part], sall.at[k, :, :, :, part],
                               fe_s.at[k - 1], fe_r.at[k - 1], (s, c, zmod(z + k)))
-            post(True, build)
-
-    def pass_rows():
-        for k in range(1, Z):
-            there = sall.at[k, :, :, :, scols(s)]
-            remote(there, there, fe_s.at[k - 1], fe_r.at[k - 1], (s, c, zmod(z - k))).wait_recv()
+            post(cond, build)
+
+    def pass_rows(zero):
+        def take():
+            for k in range(1, Z):
+                there = sall.at[k, :, :, :, portion(s, zero)]
+                remote(there, there, fe_s.at[k - 1], fe_r.at[k - 1], (s, c, zmod(z - k))).wait_recv()
+        cond = s == 0 if zero else s > 0
+        pl.when(cond)(take)
         for k in range(1, S):
             def build(k=k):
-                there = sall.at[pl.ds(1, Z - 1), :, :, :, scols(s)]
+                there = sall.at[pl.ds(1, Z - 1), :, :, :, portion(s, zero)]
                 return remote(there, there, fp_s.at[k - 1], fp_r.at[k - 1],
                               (lax.rem(s + k, S), c, z))
-            post(True, build)
+            post(cond, build)
 
     def student():
         for k in range(1, S):
             where = lax.rem(s + S - k, S)
-            there = sall.at[pl.ds(1, Z - 1), :, :, :, scols(where)]
-            remote(there, there, fp_s.at[k - 1], fp_r.at[k - 1], (where, c, z)).wait_recv()
-        load_head.wait()
+
+            def arrive(zero, k=k, where=where):
+                there = sall.at[pl.ds(1, Z - 1), :, :, :, portion(where, zero)]
+                remote(there, there, fp_s.at[k - 1], fp_r.at[k - 1], (where, c, z)).wait_recv()
+            pl.when(where == 0)(functools.partial(arrive, True))
+            pl.when(where > 0)(functools.partial(arrive, False))
 
         def one(k, carry):
             rows = layer_norm(sall[k].astype(F32).reshape(T * M * share, sw), sgain_ref[...])
@@ -187,16 +211,17 @@
 
         lax.fori_loop(0, Z, one, 0)
 
-    def spread(t):
+    def spread(t, at_root):
         def take():
             there = tbuf.at[t, c, 0]
             remote(there, there, tg_s.at[t, 0], tg_r.at[t], (root, c, z)).wait_recv()
-        pl.when(s != root)(take)
+        if not at_root:
+            pl.when(s != root)(take)
         for k in range(1, Z):
             def build(k=k):
                 return remote(tbuf.at[t, c, 0], tbuf.at[t, c, k], er_s.at[t, k - 1],
                               er_r.at[t, k - 1], (s, c, zmod(z + k)))
-            post(True, build)
+            post(s == root if at_root else s != root, build)
 
     def relay(t):
         for k in range(Z):
@@ -211,6 +236,12 @@
                                   (s, lax.rem(c + dm, M), z))
                 post(True, build)
 
+    gw = block // out_sem.shape[0]
+
+    def save_grad(j):
+        at = pl.ds(j * gw, gw)
+        return pltpu.make_async_copy(grad.at[:, at], grad_ref.at[:, at], out_sem.at[j])
+
     def gradient(t):
         for dm in range(1, M):
             for k in range(Z):
@@ -225,18 +256,54 @@
             return carry
 
         lax.fori_loop(0, Z, one, 0)
-        term = lax.dot_general(
-            fown[:, t].reshape(Z * M * share, fw), errs[...].reshape(Z * M * share, block),
-            (((0,), (0,)), ((), ())), preferred_element_type=F32,
-        )
-        if t == 0:
-            grad_ref[...] = term
-        else:
-            grad_ref[...] += term
+        feats = fown[:, t].reshape(Z * M * share, fw)
+        for j in range(block // gw):
+            at = slice(j * gw, (j + 1) * gw)
+            term = lax.dot_general(
+                feats, errs[:, :, at].reshape(Z * M * share, gw),
+                (((0,), (0,)), ((), ())), preferred_element_type=F32,
+            )
+            if t == 0:
+                grad[:, at] = term
+            else:
+                grad[:, at] += term
+            if t == T - 1:
+                save_grad(j).start()
+
+    def turned(t):
+        return root - (T - 1) + t
+
+    def forward(t):
+        cond = jnp.logical_and(s >= t, s + 1 <= turned(t + 1))
+        for r in range(turns):
+            at = pl.ds(r * turn_rows, turn_rows)
+
+            def take(r=r, at=at):
+                for k in range(1, Z):
+                    there = det.at[t, at, cols(zmod(z - k))]
+                    remote(there, there, dz_s.at[t, k - 1, r], dz_r.at[t, k - 1, r],
+                           (s, c, zmod(z - k))).wait_recv()
+
+            def build(r=r, at=at):
+                return remote(det.at[t, at, :],
+                              xfull.at[t, pl.ds(straight + r * turn_rows, turn_rows), :],
+                              dx_s.at[t, r], dx_r.at[t, r], (s + 1, c, z))
+            pl.when(cond)(take)
+            post(cond, build)
 
     def gather_state(t, active):
+        all_straight = turned(t) < root
+
         def piece(r, origin):
-            return xfull.at[t - 1, pl.ds(r * step_rows, step_rows), cols(origin)]
+            low, size = pieces[r]
+            return xfull.at[t - 1, pl.ds(low, size), cols(origin)]
+
+        def used(r):
+            if pieces[r][0] < straight:
+                return active
+            return jnp.logical_and(active, s > turned(t))
+
+        numbers = [r for r in range(len(pieces)) if pieces[r][0] < straight or all_straight]
 
         def to_right(r, k):
             there = piece(r, z - k)
@@ -256,30 +323,44 @@
             remote(there, there, al_s.at[t - 1, k - 1, r], al_r.at[t - 1, k - 1, r],
                    (s, c, z + 1)).wait_recv()
 
-        for r in range(R):
+        if t > 1:
+            forward(t - 1)
+        for r in numbers:
             def first(r=r):
                 there = piece(r, z)
                 remote(there, there, sh_s.at[t - 1, r], sh_r.at[t - 1, r],
                        (s - 1, c, z)).wait_recv()
-            pl.when(active)(first)
-            post(jnp.logical_and(active, z < Z - 1), functools.partial(to_right, r, 0))
-            post(jnp.logical_and(active, z > 0), functools.partial(to_left, r, 0))
+            pl.when(used(r))(first)
+            post(jnp.logical_and(used(r), z < Z - 1), functools.partial(to_right, r, 0))
+            post(jnp.logical_and(used(r), z > 0), functools.partial(to_left, r, 0))
+        if t == 1:
+            forward(0)
         for k in range(1, Z):
-            for r in range(R):
-                pl.when(jnp.logical_and(active, z >= k))(functools.partial(right_from, r, k))
+            for r in numbers:
+                pl.when(jnp.logical_and(used(r), z >= k))(functools.partial(right_from, r, k))
                 if k < Z - 1:
-                    post(jnp.logical_and(active, jnp.logical_and(z >= k, z < Z - 1)),
+                    post(jnp.logical_and(used(r), jnp.logical_and(z >= k, z < Z - 1)),
                          functools.partial(to_right, r, k))
-                pl.when(jnp.logical_and(active, z + k < Z))(functools.partial(left_from, r, k))
+                pl.when(jnp.logical_and(used(r), z + k < Z))(functools.partial(left_from, r, k))
                 if k < Z - 1:
-                    post(jnp.logical_and(active, jnp.logical_and(z + k < Z, z > 0)),
+                    post(jnp.logical_and(used(r), jnp.logical_and(z + k < Z, z > 0)),
                          functools.partial(to_left, r, k))
+
+        def landed():
+            for r in range(turns):
+                there = xfull.at[t - 1, pl.ds(straight + r * turn_rows, turn_rows), :]
+                remote(there, there, dx_s.at[t - 1, r], dx_r.at[t - 1, r],
+                       (s - 1, c, z)).wait_recv()
+        pl.when(jnp.logical_and(active, s <= turned(t)))(landed)
 
     def mix_cols(index):
         return pl.ds(pl.multiple_of(index * wid, 128), wid)
 
     def mixing(t):
         source = x_ref if t == 0 else xfull.at[t - 1]
+        if t == 0:
+            for copy in load_x:
+                copy.wait()
 
         def norm_rows(i, carry):
             rows = pl.ds(pl.multiple_of(i * LN_ROWS, LN_ROWS), LN_ROWS)
@@ -319,16 +400,29 @@
         summed = own.astype(F32) + jnp.dot(mixfull[t], wofull[...], preferred_element_type=F32)
         if t < T - 1:
             xs[t] = summed.astype(BF16)
+            det[t, :, cols(z)] = summed[straight:].astype(BF16)
         xrows[t] = summed.reshape(Z, share, cw).astype(BF16)
 
     def send_state(t, active):
         if t < T - 1:
-            for r in range(R):
-                def build(r=r):
-                    at = pl.ds(r * step_rows, step_rows)
+            go = jnp.logical_and(active, s < root)
+            bend = jnp.logical_and(go, s + 1 <= turned(t + 1))
+            for r in range(turns):
+                for k in range(1, Z):
+                    def build_turn(r=r, k=k):
+                        there = det.at[t, pl.ds(r * turn_rows, turn_rows), cols(z)]
+                        return remote(there, there, dz_s.at[t, k - 1, r], dz_r.at[t, k - 1, r],
+                                      (s, c, zmod(z + k)))
+                    post(bend, build_turn)
+            for r, (low, size) in enumerate(pieces):
+                def build(r=r, low=low, size=size):
+                    at = pl.ds(low, size)
                     return remote(xs.at[t, at, :], xfull.at[t, at, cols(z)],
                                   sh_s.at[t, r], sh_r.at[t, r], (s + 1, c, z))
-                post(jnp.logical_and(active, s < root), build)
+                if low < straight:
+                    post(go, build)
+                elif turned(t + 1) < root:
+                    post(jnp.logical_and(go, s + 1 > turned(t + 1)), build)
         else:
             for k in range(Z):
                 def build(k=k):
@@ -360,37 +454,51 @@
                               tg_s.at[t, to], tg_r.at[t], (jnp.int32(to), c, z))
             post(s == root, build)
 
+    def nothing():
+        advbuf[...] = jnp.zeros_like(advbuf)
+        save_adv.start()
+
     for t in range(T):
         active = True if t == 0 else s >= t
         if t == 0:
             mixing(0)
         else:
             gather_state(t, active)
+            finish(t - 1)
+            spread(t - 1, True)
             if t == 1:
-                pass_rows()
-            else:
-                relay(t - 2)
-                spread(t - 1)
+                spread_rows(False)
             pl.when(active)(functools.partial(mixing, t))
         send_mixed(t, active)
         if t == 0:
-            spread_rows()
+            pl.when(s < T)(nothing)
             gather_wo()
             project(0)
         else:
-            if t == 1:
-                spread(0)
             if t == T - 1:
-                relay(t - 1)
-                student()
+                for before in range(1, t):
+                    spread(before, False)
+                load_head.wait()
+                pl.when(s != root)(student)
+                for before in range(t):
+                    relay(before)
             pl.when(active)(functools.partial(project, t))
         send_state(t, active)
-        if t == T - 1:
-            for before in range(t):
-                gradient(before)
-        finish(t)
-
-    spread(T - 1)
+        if t == 0:
+            load_rows.wait()
+            spread_rows(True)
+        elif t == 1:
+            if t < T - 1:
+                spread(0, False)
+            pass_rows(True)
+            pass_rows(False)
+
+    finish(T - 1)
+    spread(T - 1, True)
+    pl.when(s == root)(student)
+    for before in range(T - 1):
+        gradient(before)
+    spread(T - 1, False)
     relay(T - 1)
     gradient(T - 1)
 
@@ -398,13 +506,12 @@
         for k in range(Z):
             there = advbuf.at[:, cols(zmod(z - k))]
             remote(there, there, ad_s.at[k], ad_r.at[k], (s - 1, c, zmod(z - k))).wait_recv()
-        adv_ref[...] = advbuf[...]
-
-    def nothing():
-        adv_ref[...] = jnp.zeros_like(adv_ref)
+        save_adv.start()
 
     pl.when(s >= T)(arrived)
-    pl.when(s < T)(nothing)
+    save_adv.wait()
+    for j in range(block // gw):
+        save_grad(j).wait()
     for cond, build in sends:
         if cond is True:
             build().wait_send()
@@ -423,19 +530,22 @@
         T, share = student_rows.shape[1], tokens // Z
         sw, block = w_head.shape[1:]
         cw, fw = model // Z, sw // Z
-        R = 4 if Z <= 4 else 2
+        grain = tokens // 8
+        straight, turns = 5 * grain, 3
+        pieces = ((0, 2 * grain), (2 * grain, 2 * grain), (4 * grain, grain), (straight, 3 * grain))
+        R = len(pieces)
         vmem = pl.BlockSpec(memory_space=pltpu.VMEM)
         hbm = pl.BlockSpec(memory_space=pl.ANY)
         dma = pltpu.SemaphoreType.DMA
         K = max(Z - 1, 1)
         adv, grad = pl.pallas_call(
-            functools.partial(window_kernel, S, M, Z, T, R),
+            functools.partial(window_kernel, S, M, Z, T, pieces, turns),
             out_shape=(
                 jax.ShapeDtypeStruct((share, model), BF16),
                 jax.ShapeDtypeStruct((fw, block), F32),
             ),
-            in_specs=[vmem, vmem, vmem, hbm, hbm, vmem, vmem, vmem, hbm],
-            out_specs=(vmem, vmem),
+            in_specs=[hbm, vmem, vmem, hbm, hbm, vmem, hbm, vmem, hbm],
+            out_specs=(hbm, hbm),
             scratch_shapes=[
                 pltpu.VMEM((3, model, wid), BF16),
                 pltpu.VMEM((Z * wid, cw), BF16),
@@ -453,7 +563,10 @@
                 pltpu.VMEM((Z, T, M, share, block), F32),
                 pltpu.VMEM((Z, T, M * share, fw), BF16),
                 pltpu.VMEM((Z, M * share, block), BF16),
-                dma((3,)),
+                pltpu.VMEM((tokens, model), BF16),
+                pltpu.VMEM((fw, block), F32),
+                pltpu.VMEM((T - 1, tokens - straight, model), BF16),
+                dma((5,)), dma((4,)), dma((4 if block % 512 == 0 else 1,)),
                 dma((K,)), dma((K,)), dma((K,)), dma((K,)),
                 dma((T, K)), dma((T, K)),
                 dma((T - 1, R)), dma((T - 1, R)),
@@ -465,6 +578,7 @@
                 dma((K,)), dma((K,)), dma((S,)), dma((S,)),
                 dma((T, K)), dma((T, K)),
                 dma((T, M, Z)), dma((T, M, Z)),
+                dma((T - 1, K, turns)), dma((T - 1, K, turns)), dma((T - 1, turns)), dma((T - 1, turns)),
             ],
             compiler_params=pltpu.CompilerParams(
                 collective_id=0, has_side_effects=True, vmem_limit_bytes=58 << 20

time: 140 us -> 133 us (0.950)
  Pallas kernels: 136 us -> 129 us
    pallas_call x1, Pallas kernels: 136 us -> 129 us  [on_device(): pl.pallas_call(functools.partial(window_kernel, S, M, Z, T, pieces, turns...]
where the time goes in v1:
time: 133 us
  Pallas kernels  129 us (97%)
  local copies, waits for them, and re-layouts  3.98 us (3%)
    pallas_call x1, Pallas kernels, on_device(): pl.pallas_call(functools.partial(window_kernel, S, M, Z, T, pieces, turns...  129 us
    unnamed x2, local copies, waits for them, and re-layouts  3.98 us

profile of v1, /device:TPU:1, one launch (start us, length us, event | category | flops | bytes accessed | tf_op | source)
XLA Modules:
  0.0 133.2 jit_solution(2618281425744052502)
XLA Ops:
  0.6 128.6 %shard_map.104 = (bf16[32,4096]{1,0:T(8,128)(2,1)}, f32[256,1024]{1,0:T(8,128)}) custom-call(bf16[128,4096]{1,0:T(8,128)(2,1)} %bitcast.13, s32[4,1,128]{2,1,0:T(1,128)} %seg_ref.1, f32[1,4096]{1,0:T(1,128)} %gain_ref.1, bf16[3,4096,256]{2,1,0:T(8,128)(2,1)} %bitcast.10, bf16[256,4096]{1,0:T(8,128)(2,1)} %bitcast.11, f32[1,4096]{1,0:T(1,128)} %bitcast.17, ...), custom_call_target="tpu_custom_call" | custom-call | tf_op jit(solution)/shard_map/pallas_call | solution.py:541
  129.2 1.7 %copy.13 = bf16[1,1,32,4096]{3,2,1,0:T(8,128)(2,1)} copy(bf16[1,1,32,4096]{3,2,1,0:T(8,128)(2,1)} %bitcast.16) | data formatting | bytes 524288
  130.9 2.3 %copy.14 = f32[1,256,1024]{2,1,0:T(8,128)} copy(f32[1,256,1024]{2,1,0:T(8,128)} %bitcast.14) | data formatting | bytes 2097152

commit v2 on v1

v2 whole, which is shorter than its diff:
```python
import functools

import jax
import jax.numpy as jnp
from jax import lax
from jax.experimental import pallas as pl
from jax.experimental.pallas import tpu as pltpu
from jax.sharding import PartitionSpec as P

HEAD_SIZE = 128
LN_ROWS = 16
BF16 = jnp.bfloat16
F32 = jnp.float32
MESH = pl.DeviceIdType.MESH


def layer_norm(rows, gain):
    rows = rows.astype(F32)
    centred = rows - jnp.mean(rows, axis=-1, keepdims=True)
    spread = jnp.mean(centred * centred, axis=-1, keepdims=True)
    return centred * lax.rsqrt(spread + 1e-06) * gain


def attend(query, keys, values, same):
    scores = lax.dot_general(
        query, keys, (((1,), (1,)), ((), ())), preferred_element_type=F32
    ) * HEAD_SIZE ** (-0.5)
    scores = jnp.where(same, scores, -1e30)
    top = jnp.max(scores, axis=-1, keepdims=True)
    expo = jnp.exp(scores - top)
    probs = (expo / jnp.sum(expo, axis=-1, keepdims=True)).astype(BF16)
    return jnp.dot(probs, values, preferred_element_type=F32).astype(BF16)


def window_kernel(
    S, M, Z, T, pieces, turns,
    x_hbm, seg_ref, gain_ref, wqkv_ref, wout_ref, fgain_ref, srows_ref, sgain_ref, whead_ref,
    adv_ref, grad_ref,
    wqkv, wofull, whead, normed, xfull, mixfull, xs, xrows, fin, tg, tbuf, advbuf,
    sall, pred, fown, errs, x_ref, grad, det,
    local_sem, x_sem, out_sem, wo_s, wo_r, wf_s, wf_r, mx_s, mx_r, sh_s, sh_r, ar_s, ar_r, al_s, al_r,
    ro_s, ro_r, ad_s, ad_r, tg_s, tg_r, fe_s, fe_r, fp_s, fp_r,
    er_s, er_r, ml_s, ml_r, dz_s, dz_r, dx_s, dx_r,
):
    s = lax.axis_index("section")
    c = lax.axis_index("student")
    z = lax.axis_index("dp")
    root = S - 1
    tokens, model = x_ref.shape
    wid = wout_ref.shape[0]
    share = tokens // Z
    cw = model // Z
    block = whead_ref.shape[1]
    sw = whead_ref.shape[0]
    fw = sw // Z
    straight = tokens - det.shape[1]
    turn_rows = det.shape[1] // turns
    halves = 2 if M % 2 == 0 else 1
    part = c % halves
    hw = wid // halves
    sends = []
    owners = tuple(t if t < T - 1 and t < root else root for t in range(T))

    def remote(src, dst, send, recv, where):
        return pltpu.make_async_remote_copy(
            src_ref=src, dst_ref=dst, send_sem=send, recv_sem=recv,
            device_id=where, device_id_type=MESH,
        )

    def go(cond, build):
        if cond is True:
            build().start()
        else:
            pl.when(cond)(lambda: build().start())

    def owe(cond, ref, sem):
        sends.append((cond, lambda: remote(ref, ref, sem, sem, (s, c, zmod(z + 1)))))

    def landed(ref, sem):
        remote(ref, ref, sem, sem, (s, c, zmod(z + 1))).wait_recv()

    def post(cond, build):
        go(cond, build)
        sends.append((cond, build))

    def zmod(value):
        return lax.rem(value + Z, Z)

    def cols(index):
        return pl.ds(pl.multiple_of(index * cw, 128), cw)

    load_qkv = pltpu.make_async_copy(wqkv_ref, wqkv, local_sem.at[0])
    load_head = pltpu.make_async_copy(whead_ref, whead, local_sem.at[1])
    own_wo = pltpu.make_async_copy(
        wout_ref.at[:, cols(z)],
        wofull.at[pl.ds(pl.multiple_of(z * wid, wid), wid), :],
        local_sem.at[2],
    )
    xr = tokens // x_sem.shape[0]
    load_x = [
        pltpu.make_async_copy(
            x_hbm.at[pl.ds(i * xr, xr), :], x_ref.at[pl.ds(i * xr, xr), :], x_sem.at[i]
        )
        for i in range(x_sem.shape[0])
    ]
    load_rows = pltpu.make_async_copy(srows_ref, sall.at[0], local_sem.at[3])
    save_adv = pltpu.make_async_copy(advbuf, adv_ref, local_sem.at[4])

    barrier = pltpu.get_barrier_semaphore()

    def greet(where):
        pl.semaphore_signal(barrier, inc=1, device_id=where, device_id_type=MESH)

    for at in range(S):
        for k in range(Z):
            if k:
                greet((jnp.int32(at), c, zmod(z + k)))
            else:
                pl.when(s != at)(functools.partial(greet, (jnp.int32(at), c, z)))
        for dm in range(1, M):
            greet((jnp.int32(at), lax.rem(c + dm, M), z))
    for copy in load_x:
        copy.start()
    load_qkv.start()
    own_wo.start()
    load_rows.start()
    load_head.start()
    pl.semaphore_wait(barrier, S * Z - 1 + S * (M - 1))

    def wo_rows(source, which):
        return pl.ds(pl.multiple_of(source * wid + which * hw, hw), hw)

    for k in sorted(range(1, Z), reverse=True):
        def build(k=k):
            to = zmod(z + k)
            return remote(
                wout_ref.at[pl.ds(pl.multiple_of(part * hw, hw), hw), cols(to)],
                wofull.at[wo_rows(z, part), :],
                wo_s.at[0], wo_r.at[k - 1], (s, c, to),
            )
        go(True, build)
    owe(True, wofull.at[pl.ds(0, (Z - 1) * hw), :], wo_s.at[0])

    def pass_on(k):
        source = zmod(z - k)
        mine = wofull.at[wo_rows(source, part), :]
        mate = c + 1 - 2 * part
        return remote(mine, mine, wf_s.at[0], wf_r.at[k - 1], (s, mate, z))

    def gather_wo():
        for k in range(1, Z):
            source = zmod(z - k)
            mine = wofull.at[wo_rows(source, part), :]
            landed(mine, wo_r.at[k - 1])
            if halves == 2:
                go(True, functools.partial(pass_on, k))
        if halves == 2:
            owe(True, wofull.at[pl.ds(0, (Z - 1) * hw), :], wf_s.at[0])
            for k in range(1, Z):
                source = zmod(z - k)
                other = wofull.at[wo_rows(source, 1 - part), :]
                landed(other, wf_r.at[k - 1])
        own_wo.wait()

    def spread_rows():
        for k in range(1, Z):
            def build(k=k):
                return remote(srows_ref, sall.at[k], fe_s.at[0], fe_r.at[k - 1],
                              (s, c, zmod(z + k)))
            go(s == 0, build)
        owe(s == 0, sall.at[pl.ds(0, Z - 1)], fe_s.at[0])

    handed = (1,) if root > 1 else ()

    def pass_rows():
        for k in range(1, Z):
            pl.when(s == 0)(functools.partial(landed, sall.at[k], fe_r.at[k - 1]))
            for to in range(S - 1, 0, -1):
                def build(k=k, to=to):
                    there = sall.at[k]
                    return remote(there, there, fp_s.at[k - 1, to - 1], fp_r.at[k - 1],
                                  (jnp.int32(to), c, z))
                if to != root or k not in handed:
                    post(s == 0, build)

    def hand_rows():
        for k in handed:
            there = sall.at[k]

            def build(k=k, there=there):
                return remote(there, there, fp_s.at[k - 1, root - 1], fp_r.at[k - 1],
                              (jnp.int32(root), c, z))
            pl.when(s == 1)(functools.partial(landed, there, fp_r.at[k - 1]))
            post(s == 1, build)

    def student():
        for k in range(1, Z):
            pl.when(s > 1 if k in handed else s > 0)(
                functools.partial(landed, sall.at[k], fp_r.at[k - 1])
            )

        def one(k, carry):
            rows = layer_norm(sall[k].astype(F32).reshape(T * M * share, sw), sgain_ref[...])
            rows = rows.astype(BF16)
            for zz in range(Z):
                def own(zz=zz):
                    fown[k] = rows[:, zz * fw:(zz + 1) * fw].reshape(T, M * share, fw)
                pl.when(z == zz)(own)
            pred[k] = jnp.dot(rows, whead[...], preferred_element_type=F32).reshape(
                T, M, share, block
            )
            return carry

        lax.fori_loop(0, Z, one, 0)

    def spread(t, who):
        pl.when(jnp.logical_and(who, s != owners[t]))(
            functools.partial(landed, tbuf.at[t, c, 0], tg_r.at[t])
        )
        for k in range(1, Z):
            def build(k=k):
                return remote(tbuf.at[t, c, 0], tbuf.at[t, c, k], er_s.at[t],
                              er_r.at[t, k - 1], (s, c, zmod(z + k)))
            go(who, build)
        owe(who, tbuf.at[t, c, pl.ds(0, Z - 1)], er_s.at[t])

    def relay(t):
        for k in range(Z):
            there = tbuf.at[t, c, k]
            if k:
                landed(there, er_r.at[t, k - 1])
            for dm in range(1, M):
                def build(k=k, dm=dm):
                    there = tbuf.at[t, c, k]
                    return remote(there, there, ml_s.at[t], ml_r.at[t, dm - 1],
                                  (s, lax.rem(c + dm, M), z))
                go(True, build)
        if M > 1:
            owe(True, tbuf.at[t, pl.ds(0, M - 1)], ml_s.at[t])

    gw = block // out_sem.shape[0]

    def save_grad(j):
        at = pl.ds(j * gw, gw)
        return pltpu.make_async_copy(grad.at[:, at], grad_ref.at[:, at], out_sem.at[j])

    def gradient(t):
        for dm in range(1, M):
            landed(tbuf.at[t, lax.rem(c + M - dm, M)], ml_r.at[t, dm - 1])

        def one(k, carry):
            err = (pred[k, t] - tbuf[t, :, k].astype(F32)) * (2.0 / tokens)
            errs[k] = err.reshape(M * share, block).astype(BF16)
            return carry

        lax.fori_loop(0, Z, one, 0)
        feats = fown[:, t].reshape(Z * M * share, fw)
        for j in range(block // gw):
            at = slice(j * gw, (j + 1) * gw)
            term = lax.dot_general(
                feats, errs[:, :, at].reshape(Z * M * share, gw),
                (((0,), (0,)), ((), ())), preferred_element_type=F32,
            )
            if t == 0:
                grad[:, at] = term
            else:
                grad[:, at] += term
            if t == T - 1:
                save_grad(j).start()

    def turned(t):
        return root - (T - 1) + t

    def forward(t):
        cond = jnp.logical_and(s >= t, s + 1 <= turned(t + 1))
        for r in range(turns):
            at = pl.ds(r * turn_rows, turn_rows)

            def build(r=r, at=at):
                return remote(det.at[t, at, :],
                              xfull.at[t, pl.ds(straight + r * turn_rows, turn_rows), :],
                              dx_s.at[t], dx_r.at[t, r], (s + 1, c, z))
            whole = det.at[t, at, pl.ds(0, (Z - 1) * cw)]
            pl.when(cond)(functools.partial(landed, whole, dz_r.at[t, r]))
            go(cond, build)
        owe(cond, det.at[t], dx_s.at[t])

    def gather_state(t, active):
        all_straight = turned(t) < root

        def piece(r, origin):
            low, size = pieces[r]
            return xfull.at[t - 1, pl.ds(low, size), cols(origin)]

        def used(r):
            if pieces[r][0] < straight:
                return active
            return jnp.logical_and(active, s > turned(t))

        numbers = [r for r in range(len(pieces)) if pieces[r][0] < straight or all_straight]

        def to_right(r, k):
            there = piece(r, z - k)
            return remote(there, there, ar_s.at[t - 1, k, part_of(r)], ar_r.at[t - 1, k, r],
                          (s, c, z + 1))

        def to_left(r, k):
            there = piece(r, z + k)
            return remote(there, there, al_s.at[t - 1, k, part_of(r)], al_r.at[t - 1, k, r],
                          (s, c, z - 1))

        def part_of(r):
            return 0 if pieces[r][0] < straight else 1

        def send(cond, build, r, k, sem):
            go(jnp.logical_and(used(r), cond), functools.partial(build, r, k))
            size = straight if r == 0 else tokens - straight
            if r == 0 or part_of(r):
                owe(jnp.logical_and(used(r), cond),
                    xfull.at[t - 1, pl.ds(0, size), pl.ds(0, cw)], sem.at[t - 1, k, part_of(r)])

        for r in numbers:
            pl.when(used(r))(functools.partial(landed, piece(r, z), sh_r.at[t - 1, r]))
            send(z < Z - 1, to_right, r, 0, ar_s)
            send(z > 0, to_left, r, 0, al_s)
        if t == 1:
            forward(0)
        for k in range(1, Z):
            for r in numbers:
                pl.when(jnp.logical_and(used(r), z >= k))(
                    functools.partial(landed, piece(r, z - k), ar_r.at[t - 1, k - 1, r])
                )
                if k < Z - 1:
                    send(jnp.logical_and(z >= k, z < Z - 1), to_right, r, k, ar_s)
                pl.when(jnp.logical_and(used(r), z + k < Z))(
                    functools.partial(landed, piece(r, z + k), al_r.at[t - 1, k - 1, r])
                )
                if k < Z - 1:
                    send(jnp.logical_and(z + k < Z, z > 0), to_left, r, k, al_s)

        def turned_in():
            for r in range(turns):
                landed(xfull.at[t - 1, pl.ds(straight + r * turn_rows, turn_rows), :],
                       dx_r.at[t - 1, r])
        pl.when(jnp.logical_and(active, s <= turned(t)))(turned_in)

    def mix_cols(index):
        return pl.ds(pl.multiple_of(index * wid, 128), wid)

    def mixing(t):
        source = x_ref if t == 0 else xfull.at[t - 1]
        if t == 0:
            for copy in load_x:
                copy.wait()

        def norm_rows(i, carry):
            rows = pl.ds(pl.multiple_of(i * LN_ROWS, LN_ROWS), LN_ROWS)
            normed[rows, :] = layer_norm(source[rows, :], gain_ref[...]).astype(BF16)
            return carry

        lax.fori_loop(0, tokens // LN_ROWS, norm_rows, 0)
        if t == 0:
            load_qkv.wait()
        rows = normed[...]
        query, keys, values = [
            jnp.dot(rows, wqkv[j], preferred_element_type=F32).astype(BF16)
            for j in range(3)
        ]
        crops = jnp.broadcast_to(seg_ref[s - t].astype(F32), (tokens, tokens))
        same = crops == crops.T
        outs = []
        for h in range(wid // HEAD_SIZE):
            at = slice(h * HEAD_SIZE, (h + 1) * HEAD_SIZE)
            outs.append(attend(query[:, at], keys[:, at], values[:, at], same))
        mixfull[t, :, mix_cols(z)] = jnp.concatenate(outs, axis=1)

    def send_mixed(t, active):
        for k in range(1, Z):
            def build(k=k):
                own = mixfull.at[t, :, mix_cols(z)]
                return remote(own, own, mx_s.at[t], mx_r.at[t], (s, c, zmod(z + k)))
            go(active, build)
        owe(active, mixfull.at[t, :, pl.ds(0, (Z - 1) * wid)], mx_s.at[t])

    def project(t):
        landed(mixfull.at[t, :, pl.ds(0, (Z - 1) * wid)], mx_r.at[t])
        own = x_ref[:, cols(z)] if t == 0 else xfull[t - 1, :, cols(z)]
        summed = own.astype(F32) + jnp.dot(mixfull[t], wofull[...], preferred_element_type=F32)
        if t < T - 1:
            xs[t] = summed.astype(BF16)
            det[t, :, cols(z)] = summed[straight:].astype(BF16)
        xrows[t] = summed.reshape(Z, share, cw).astype(BF16)

    def send_state(t, active):
        if t < T - 1:
            go_on = jnp.logical_and(active, s < root)
            bend = jnp.logical_and(go_on, s + 1 <= turned(t + 1))
            for r in range(turns):
                for k in range(1, Z):
                    def build_turn(r=r, k=k):
                        there = det.at[t, pl.ds(r * turn_rows, turn_rows), cols(z)]
                        return remote(there, there, dz_s.at[t], dz_r.at[t, r],
                                      (s, c, zmod(z + k)))
                    go(bend, build_turn)
            owe(bend, det.at[t, :, pl.ds(0, (Z - 1) * cw)], dz_s.at[t])
            for r, (low, size) in enumerate(pieces):
                def build(r=r, low=low, size=size):
                    at = pl.ds(low, size)
                    return remote(xs.at[t, at, :], xfull.at[t, at, cols(z)],
                                  sh_s.at[t, 0 if low < straight else 1], sh_r.at[t, r],
                                  (s + 1, c, z))
                if low < straight:
                    go(go_on, build)
                elif turned(t + 1) < root:
                    post(jnp.logical_and(go_on, s + 1 > turned(t + 1)), build)
            owe(go_on, xs.at[t, pl.ds(0, straight), :], sh_s.at[t, 0])
        else:
            for k in range(Z):
                def build(k=k):
                    to = zmod(z + k)
                    return remote(xrows.at[t, to], advbuf.at[:, cols(z)],
                                  ad_s.at[0], ad_r.at[0], (s + 1, c, to))
                go(jnp.logical_and(active, s < root), build)
            owe(jnp.logical_and(active, s < root), advbuf, ad_s.at[0])
        low = 0 if owners[t] != root else 1
        for k in range(low, Z):
            def build_row(k=k):
                to = zmod(z + k)
                return remote(xrows.at[t, to], fin.at[t, :, cols(z)],
                              ro_s.at[t], ro_r.at[t], (jnp.int32(owners[t]), c, to))
            go(s == root, build_row)
        owe(s == root, fin.at[t, :, pl.ds(0, (Z - low) * cw)], ro_s.at[t])

    def finish(t):
        own = owners[t]

        def rows():
            if own == root:
                fin[t, :, cols(z)] = xrows[t, z]
            landed(fin.at[t, :, pl.ds(0, (Z - (own == root)) * cw)], ro_r.at[t])
            tg[t] = layer_norm(fin[t], fgain_ref[...]).astype(BF16)
            tbuf[t, c, 0] = tg[t, :, own * block:(own + 1) * block]

        pl.when(s == own)(rows)
        for to in range(S):
            if to != own:
                def build(to=to):
                    return remote(tg.at[t, :, to * block:(to + 1) * block], tbuf.at[t, c, 0],
                                  tg_s.at[t], tg_r.at[t], (jnp.int32(to), c, z))
                go(s == own, build)
        owe(s == own, tg.at[t, :, pl.ds(0, (S - 1) * block)], tg_s.at[t])

    def nothing():
        advbuf[...] = jnp.zeros_like(advbuf)
        save_adv.start()

    last, others = s == root, s != root
    for t in range(T):
        active = True if t == 0 else s >= t
        if t == 0:
            mixing(0)
        elif t == 1:
            finish(0)
            gather_state(1, active)
            spread_rows()
            pass_rows()
            spread(0, last)
            pl.when(active)(functools.partial(mixing, t))
        else:
            if t == T - 1:
                hand_rows()
            forward(t - 1)
            gather_state(t, jnp.logical_and(active, others))
            pl.when(active)(functools.partial(mixing, t))
        send_mixed(t, active)
        if t == 0:
            pl.when(s < T)(nothing)
            gather_wo()
            project(0)
        else:
            if t < T - 1:
                gather_state(t + 1, last)
            else:
                load_head.wait()
                for before in range(1, t):
                    finish(before)
                    spread(before, others)
                relay(0)
            pl.when(active)(functools.partial(project, t))
        send_state(t, active)
        if t == 0:
            load_rows.wait()
        elif t == 1:
            spread(0, others)

    finish(T - 1)
    spread(T - 1, last)
    for before in range(1, T - 1):
        spread(before, last)
    spread(T - 1, others)
    student()
    for before in range(1, T - 1):
        relay(before)
    for before in range(T - 1):
        gradient(before)
    relay(T - 1)
    gradient(T - 1)

    def arrived():
        landed(advbuf, ad_r.at[0])
        save_adv.start()

    pl.when(s >= T)(arrived)
    save_adv.wait()
    for j in range(block // gw):
        save_grad(j).wait()
    for cond, build in sends:
        if cond is True:
            build().wait_send()
        else:
            pl.when(cond)(lambda build=build: build().wait_send())


def solution(mesh):
    S, M, Z = mesh.shape["section"], mesh.shape["student"], mesh.shape["dp"]

    def on_device(
        in_flight, segments, norm_gain, w_qkv, w_out, final_gain, student_rows, student_gain, w_head
    ):
        tokens, model = in_flight.shape[2:]
        wid = w_out.shape[1]
        T, share = student_rows.shape[1], tokens // Z
        sw, block = w_head.shape[1:]
        cw, fw = model // Z, sw // Z
        grain = tokens // 8
        straight, turns = 5 * grain, 3
        pieces = ((0, 2 * grain), (2 * grain, 2 * grain), (4 * grain, grain), (straight, 3 * grain))
        R = len(pieces)
        vmem = pl.BlockSpec(memory_space=pltpu.VMEM)
        hbm = pl.BlockSpec(memory_space=pl.ANY)
        dma = pltpu.SemaphoreType.DMA
        K = max(Z - 1, 1)
        adv, grad = pl.pallas_call(
            functools.partial(window_kernel, S, M, Z, T, pieces, turns),
            out_shape=(
                jax.ShapeDtypeStruct((share, model), BF16),
                jax.ShapeDtypeStruct((fw, block), F32),
            ),
            in_specs=[hbm, vmem, vmem, hbm, hbm, vmem, hbm, vmem, hbm],
            out_specs=(hbm, hbm),
            scratch_shapes=[
                pltpu.VMEM((3, model, wid), BF16),
                pltpu.VMEM((Z * wid, cw), BF16),
                pltpu.VMEM((sw, block), BF16),
                pltpu.VMEM((tokens, model), BF16),
                pltpu.VMEM((T - 1, tokens, model), BF16),
                pltpu.VMEM((T, tokens, Z * wid), BF16),
                pltpu.VMEM((T - 1, tokens, cw), BF16),
                pltpu.VMEM((T, Z, share, cw), BF16),
                pltpu.VMEM((T, share, model), BF16),
                pltpu.VMEM((T, share, model), BF16),
                pltpu.VMEM((T, M, Z, share, block), BF16),
                pltpu.VMEM((share, model), BF16),
                pltpu.VMEM((Z, T, M, share, sw), BF16),
                pltpu.VMEM((Z, T, M, share, block), F32),
                pltpu.VMEM((Z, T, M * share, fw), BF16),
                pltpu.VMEM((Z, M * share, block), BF16),
                pltpu.VMEM((tokens, model), BF16),
                pltpu.VMEM((fw, block), F32),
                pltpu.VMEM((T - 1, tokens - straight, model), BF16),
                dma((5,)), dma((4,)), dma((4 if block % 512 == 0 else 1,)),
                dma((1,)), dma((K,)), dma((1,)), dma((K,)),
                dma((T,)), dma((T,)),
                dma((T - 1, 2)), dma((T - 1, R)),
                dma((T - 1, K, 2)), dma((T - 1, K, R)),
                dma((T - 1, K, 2)), dma((T - 1, K, R)),
                dma((T,)), dma((T,)),
                dma((1,)), dma((1,)),
                dma((T,)), dma((T,)),
                dma((1,)), dma((K,)), dma((K, S - 1)), dma((K,)),
                dma((T,)), dma((T, K)),
                dma((T,)), dma((T, max(M - 1, 1))),
                dma((T - 1,)), dma((T - 1, turns)), dma((T - 1,)), dma((T - 1, turns)),
            ],
            compiler_params=pltpu.CompilerParams(
                collective_id=0, has_side_effects=True, vmem_limit_bytes=58 << 20
            ),
        )(
            in_flight[0, 0], segments, norm_gain, jnp.transpose(w_qkv[0], (1, 0, 2)), w_out[0],
            final_gain[None], student_rows[0], student_gain, w_head[0],
        )
        return adv[None, None], grad[None]

    in_specs = (
        P("section", "student", None, None),
        P(None, "student", None),
        P("section", None),
        P("section", None, None, "dp"),
        P("section", "dp", None),
        P(),
        P("student", None, None, "dp", None),
        P("student", None),
        P("student", None, "section"),
    )
    out_specs = (P("section", "student", "dp", None), P("student", "dp", "section"))
    return jax.shard_map(
        on_device, mesh=mesh, in_specs=in_specs, out_specs=out_specs, check_vma=False
    )
```

time: 133 us -> 133 us (level)
  the two profiles are of different devices: /device:TPU:1 before, /device:TPU:26 now
where the time goes in v2:
time: 133 us
  Pallas kernels  128 us (96%)
  local copies, waits for them, and re-layouts  3.98 us (3%)
    pallas_call x1, Pallas kernels, on_device(): pl.pallas_call(functools.partial(window_kernel, S, M, Z, T, pieces, turns...  128 us
    unnamed x2, local copies, waits for them, and re-layouts  3.98 us

profile of v2, /device:TPU:26, one launch (start us, length us, event | category | flops | bytes accessed | tf_op | source)
XLA Modules:
  0.0 132.6 jit_solution(8577080269132820428)
XLA Ops:
  0.6 128.0 %shard_map.104 = (bf16[32,4096]{1,0:T(8,128)(2,1)}, f32[256,1024]{1,0:T(8,128)}) custom-call(bf16[128,4096]{1,0:T(8,128)(2,1)} %bitcast.13, s32[4,1,128]{2,1,0:T(1,128)} %seg_ref.1, f32[1,4096]{1,0:T(1,128)} %gain_ref.1, bf16[3,4096,256]{2,1,0:T(8,128)(2,1)} %bitcast.10, bf16[256,4096]{1,0:T(8,128)(2,1)} %bitcast.11, f32[1,4096]{1,0:T(1,128)} %bitcast.17, ...), custom_call_target="tpu_custom_call" | custom-call | tf_op jit(solution)/shard_map/pallas_call | solution.py:543
  128.7 1.7 %copy.13 = bf16[1,1,32,4096]{3,2,1,0:T(8,128)(2,1)} copy(bf16[1,1,32,4096]{3,2,1,0:T(8,128)(2,1)} %bitcast.16) | data formatting | bytes 524288
  130.3 2.3 %copy.14 = f32[1,256,1024]{2,1,0:T(8,128)} copy(f32[1,256,1024]{2,1,0:T(8,128)} %bitcast.14) | data formatting | bytes 2097152

commit v3 on v2

--- a/solution.py
+++ b/solution.py
@@ -162,40 +162,53 @@
                 landed(other, wf_r.at[k - 1])
         own_wo.wait()
 
-    def spread_rows():
-        for k in range(1, Z):
-            def build(k=k):
-                return remote(srows_ref, sall.at[k], fe_s.at[0], fe_r.at[k - 1],
-                              (s, c, zmod(z + k)))
-            go(s == 0, build)
-        owe(s == 0, sall.at[pl.ds(0, Z - 1)], fe_s.at[0])
-
-    handed = (1,) if root > 1 else ()
+    handing = root > 1
+
+    def slots(j):
+        return (z >= j, j, z < Z - 1, z + 1), (z + j < Z, (Z - j) % Z, z > 0, z - 1)
+
+    def send_rows(j):
+        for way, (here, at, more, to) in enumerate(slots(j)):
+            lands = (at + 1) % Z if way == 0 else (at + Z - 1) % Z
+
+            def build(at=at, to=to, lands=lands, way=way):
+                return remote(sall.at[at], sall.at[lands], fe_s.at[j, way], fe_r.at[lands - 1],
+                              (s, c, to))
+            post(jnp.logical_and(s == 0, jnp.logical_and(here, more)), build)
 
     def pass_rows():
-        for k in range(1, Z):
-            pl.when(s == 0)(functools.partial(landed, sall.at[k], fe_r.at[k - 1]))
-            for to in range(S - 1, 0, -1):
-                def build(k=k, to=to):
-                    there = sall.at[k]
-                    return remote(there, there, fp_s.at[k - 1, to - 1], fp_r.at[k - 1],
-                                  (jnp.int32(to), c, z))
-                if to != root or k not in handed:
-                    post(s == 0, build)
-
-    def hand_rows():
-        for k in handed:
-            there = sall.at[k]
-
-            def build(k=k, there=there):
-                return remote(there, there, fp_s.at[k - 1, root - 1], fp_r.at[k - 1],
+        send_rows(0)
+        for j in range(1, Z):
+            for here, at, more, to in slots(j):
+                mine = jnp.logical_and(s == 0, here)
+                pl.when(mine)(functools.partial(landed, sall.at[at], fe_r.at[at - 1]))
+            if j < Z - 1:
+                send_rows(j)
+            for here, at, more, to in slots(j):
+                mine = jnp.logical_and(s == 0, here)
+                for to in range(1, S):
+                    def build(at=at, to=to):
+                        there = sall.at[at]
+                        return remote(there, there, fp_s.at[at - 1, to - 1], fp_r.at[at - 1],
+                                      (jnp.int32(to), c, z))
+                    if to != root or not handing:
+                        post(mine, build)
+
+    def hand_rows(j):
+        for here, at, more, to in slots(j):
+            there = sall.at[at]
+
+            def build(at=at, there=there):
+                return remote(there, there, fp_s.at[at - 1, root - 1], fp_r.at[at - 1],
                               (jnp.int32(root), c, z))
-            pl.when(s == 1)(functools.partial(landed, there, fp_r.at[k - 1]))
-            post(s == 1, build)
+            if handing:
+                mine = jnp.logical_and(s == 1, here)
+                pl.when(mine)(functools.partial(landed, there, fp_r.at[at - 1]))
+                post(mine, build)
 
     def student():
         for k in range(1, Z):
-            pl.when(s > 1 if k in handed else s > 0)(
+            pl.when(s > 1 if handing else s > 0)(
                 functools.partial(landed, sall.at[k], fp_r.at[k - 1])
             )
 
@@ -462,14 +475,16 @@
         elif t == 1:
             finish(0)
             gather_state(1, active)
-            spread_rows()
             pass_rows()
             spread(0, last)
             pl.when(active)(functools.partial(mixing, t))
         else:
             if t == T - 1:
-                hand_rows()
+                hand_rows(1)
             forward(t - 1)
+            if t == T - 1:
+                for j in range(2, Z - 1):
+                    hand_rows(j)
             gather_state(t, jnp.logical_and(active, others))
             pl.when(active)(functools.partial(mixing, t))
         send_mixed(t, active)
@@ -486,6 +501,8 @@
                     finish(before)
                     spread(before, others)
                 relay(0)
+                if Z > 2:
+                    hand_rows(Z - 1)
             pl.when(active)(functools.partial(project, t))
         send_state(t, active)
         if t == 0:
@@ -577,7 +594,7 @@
                 dma((T,)), dma((T,)),
                 dma((1,)), dma((1,)),
                 dma((T,)), dma((T,)),
-                dma((1,)), dma((K,)), dma((K, S - 1)), dma((K,)),
+                dma((K, 2)), dma((K,)), dma((K, S - 1)), dma((K,)),
                 dma((T,)), dma((T, K)),
                 dma((T,)), dma((T, max(M - 1, 1))),
                 dma((T - 1,)), dma((T - 1, turns)), dma((T - 1,)), dma((T - 1, turns)),

time: 133 us -> 123 us (0.925)
  the two profiles are of different devices: /device:TPU:26 before, /device:TPU:1 now
where the time goes in v3:
time: 123 us; the launch traced here: 120 us
  Pallas kernels  116 us (94%)
  local copies, waits for them, and re-layouts  3.98 us (3%)
    pallas_call x1, Pallas kernels, on_device(): pl.pallas_call(functools.partial(window_kernel, S, M, Z, T, pieces, turns...  116 us
    unnamed x2, local copies, waits for them, and re-layouts  3.98 us

profile of v3, /device:TPU:1, one launch (start us, length us, event | category | flops | bytes accessed | tf_op | source)
XLA Modules:
  0.0 120.5 jit_solution(17848787790932684317)
XLA Ops:
  0.6 115.9 %shard_map.104 = (bf16[32,4096]{1,0:T(8,128)(2,1)}, f32[256,1024]{1,0:T(8,128)}) custom-call(bf16[128,4096]{1,0:T(8,128)(2,1)} %bitcast.13, s32[4,1,128]{2,1,0:T(1,128)} %seg_ref.1, f32[1,4096]{1,0:T(1,128)} %gain_ref.1, bf16[3,4096,256]{2,1,0:T(8,128)(2,1)} %bitcast.10, bf16[256,4096]{1,0:T(8,128)(2,1)} %bitcast.11, f32[1,4096]{1,0:T(1,128)} %bitcast.17, ...), custom_call_target="tpu_custom_call" | custom-call | tf_op jit(solution)/shard_map/pallas_call | solution.py:560
  116.5 1.7 %copy.13 = bf16[1,1,32,4096]{3,2,1,0:T(8,128)(2,1)} copy(bf16[1,1,32,4096]{3,2,1,0:T(8,128)(2,1)} %bitcast.16) | data formatting | bytes 524288
  118.2 2.3 %copy.14 = f32[1,256,1024]{2,1,0:T(8,128)} copy(f32[1,256,1024]{2,1,0:T(8,128)} %bitcast.14) | data formatting | bytes 2097152

commit v4 on v3

--- a/solution.py
+++ b/solution.py
@@ -37,7 +37,7 @@
     x_hbm, seg_ref, gain_ref, wqkv_ref, wout_ref, fgain_ref, srows_ref, sgain_ref, whead_ref,
     adv_ref, grad_ref,
     wqkv, wofull, whead, normed, xfull, mixfull, xs, xrows, fin, tg, tbuf, advbuf,
-    sall, pred, fown, errs, x_ref, grad, det,
+    sall, pred, fown, errs, x_ref, grad, det, slim_grad,
     local_sem, x_sem, out_sem, wo_s, wo_r, wf_s, wf_r, mx_s, mx_r, sh_s, sh_r, ar_s, ar_r, al_s, al_r,
     ro_s, ro_r, ad_s, ad_r, tg_s, tg_r, fe_s, fe_r, fp_s, fp_r,
     er_s, er_r, ml_s, ml_r, dz_s, dz_r, dx_s, dx_r,
@@ -53,6 +53,8 @@
     block = whead_ref.shape[1]
     sw = whead_ref.shape[0]
     fw = sw // Z
+    cuts = tg_r.shape[1]
+    slim = share // cuts
     straight = tokens - det.shape[1]
     turn_rows = det.shape[1] // turns
     halves = 2 if M % 2 == 0 else 1
@@ -227,27 +229,30 @@
         lax.fori_loop(0, Z, one, 0)
 
     def spread(t, who):
-        pl.when(jnp.logical_and(who, s != owners[t]))(
-            functools.partial(landed, tbuf.at[t, c, 0], tg_r.at[t])
-        )
-        for k in range(1, Z):
-            def build(k=k):
-                return remote(tbuf.at[t, c, 0], tbuf.at[t, c, k], er_s.at[t],
-                              er_r.at[t, k - 1], (s, c, zmod(z + k)))
-            go(who, build)
+        for h in range(cuts):
+            at = pl.ds(h * slim, slim)
+            pl.when(jnp.logical_and(who, s != owners[t]))(
+                functools.partial(landed, tbuf.at[t, c, 0, at], tg_r.at[t, h])
+            )
+            for k in range(1, Z):
+                def build(k=k, at=at, h=h):
+                    return remote(tbuf.at[t, c, 0, at], tbuf.at[t, c, k, at], er_s.at[t],
+                                  er_r.at[t, k - 1, h], (s, c, zmod(z + k)))
+                go(who, build)
         owe(who, tbuf.at[t, c, pl.ds(0, Z - 1)], er_s.at[t])
 
     def relay(t):
-        for k in range(Z):
-            there = tbuf.at[t, c, k]
-            if k:
-                landed(there, er_r.at[t, k - 1])
-            for dm in range(1, M):
-                def build(k=k, dm=dm):
-                    there = tbuf.at[t, c, k]
-                    return remote(there, there, ml_s.at[t], ml_r.at[t, dm - 1],
-                                  (s, lax.rem(c + dm, M), z))
-                go(True, build)
+        for h in range(cuts):
+            at = pl.ds(h * slim, slim)
+            for k in range(Z):
+                there = tbuf.at[t, c, k, at]
+                if k:
+                    landed(there, er_r.at[t, k - 1, h])
+                for dm in range(1, M):
+                    def build(there=there, dm=dm):
+                        return remote(there, there, ml_s.at[t], ml_r.at[t, dm - 1],
+                                      (s, lax.rem(c + dm, M), z))
+                    go(True, build)
         if M > 1:
             owe(True, tbuf.at[t, pl.ds(0, M - 1)], ml_s.at[t])
 
@@ -255,7 +260,7 @@
 
     def save_grad(j):
         at = pl.ds(j * gw, gw)
-        return pltpu.make_async_copy(grad.at[:, at], grad_ref.at[:, at], out_sem.at[j])
+        return pltpu.make_async_copy(slim_grad.at[:, at], grad_ref.at[:, at], out_sem.at[j])
 
     def gradient(t):
         for dm in range(1, M):
@@ -276,9 +281,10 @@
             )
             if t == 0:
                 grad[:, at] = term
+            elif t < T - 1:
+                grad[:, at] += term
             else:
-                grad[:, at] += term
-            if t == T - 1:
+                slim_grad[:, at] = (grad[:, at] + term).astype(BF16)
                 save_grad(j).start()
 
     def turned(t):
@@ -297,6 +303,16 @@
             pl.when(cond)(functools.partial(landed, whole, dz_r.at[t, r]))
             go(cond, build)
         owe(cond, det.at[t], dx_s.at[t])
+
+    def norm(t, low, size):
+        source = x_ref if t == 0 else xfull.at[t - 1]
+
+        def norm_rows(i, carry):
+            rows = pl.ds(pl.multiple_of(low + i * LN_ROWS, LN_ROWS), LN_ROWS)
+            normed[rows, :] = layer_norm(source[rows, :], gain_ref[...]).astype(BF16)
+            return carry
+
+        lax.fori_loop(0, size // LN_ROWS, norm_rows, 0)
 
     def gather_state(t, active):
         all_straight = turned(t) < root
@@ -350,28 +366,24 @@
                 )
                 if k < Z - 1:
                     send(jnp.logical_and(z + k < Z, z > 0), to_left, r, k, al_s)
+                else:
+                    pl.when(used(r))(functools.partial(norm, t, *pieces[r]))
 
         def turned_in():
             for r in range(turns):
                 landed(xfull.at[t - 1, pl.ds(straight + r * turn_rows, turn_rows), :],
                        dx_r.at[t - 1, r])
+                norm(t, straight + r * turn_rows, turn_rows)
         pl.when(jnp.logical_and(active, s <= turned(t)))(turned_in)
 
     def mix_cols(index):
         return pl.ds(pl.multiple_of(index * wid, 128), wid)
 
     def mixing(t):
-        source = x_ref if t == 0 else xfull.at[t - 1]
         if t == 0:
             for copy in load_x:
                 copy.wait()
-
-        def norm_rows(i, carry):
-            rows = pl.ds(pl.multiple_of(i * LN_ROWS, LN_ROWS), LN_ROWS)
-            normed[rows, :] = layer_norm(source[rows, :], gain_ref[...]).astype(BF16)
-            return carry
-
-        lax.fori_loop(0, tokens // LN_ROWS, norm_rows, 0)
+            norm(0, 0, tokens)
         if t == 0:
             load_qkv.wait()
         rows = normed[...]
@@ -435,32 +447,39 @@
                                   ad_s.at[0], ad_r.at[0], (s + 1, c, to))
                 go(jnp.logical_and(active, s < root), build)
             owe(jnp.logical_and(active, s < root), advbuf, ad_s.at[0])
+
+    def retire(t):
         low = 0 if owners[t] != root else 1
-        for k in range(low, Z):
-            def build_row(k=k):
-                to = zmod(z + k)
-                return remote(xrows.at[t, to], fin.at[t, :, cols(z)],
-                              ro_s.at[t], ro_r.at[t], (jnp.int32(owners[t]), c, to))
-            go(s == root, build_row)
+        for h in range(cuts):
+            at = pl.ds(h * slim, slim)
+            for k in range(low, Z):
+                def build(k=k, h=h, at=at):
+                    to = zmod(z + k)
+                    return remote(xrows.at[t, to, at], fin.at[t, at, cols(z)],
+                                  ro_s.at[t], ro_r.at[t, h], (jnp.int32(owners[t]), c, to))
+                go(s == root, build)
         owe(s == root, fin.at[t, :, pl.ds(0, (Z - low) * cw)], ro_s.at[t])
 
     def finish(t):
         own = owners[t]
-
-        def rows():
-            if own == root:
-                fin[t, :, cols(z)] = xrows[t, z]
-            landed(fin.at[t, :, pl.ds(0, (Z - (own == root)) * cw)], ro_r.at[t])
-            tg[t] = layer_norm(fin[t], fgain_ref[...]).astype(BF16)
-            tbuf[t, c, 0] = tg[t, :, own * block:(own + 1) * block]
-
-        pl.when(s == own)(rows)
-        for to in range(S):
-            if to != own:
-                def build(to=to):
-                    return remote(tg.at[t, :, to * block:(to + 1) * block], tbuf.at[t, c, 0],
-                                  tg_s.at[t], tg_r.at[t], (jnp.int32(to), c, z))
-                go(s == own, build)
+        for h in range(cuts):
+            at = pl.ds(h * slim, slim)
+
+            def rows(at=at, h=h):
+                if own == root:
+                    fin[t, at, cols(z)] = xrows[t, z, at]
+                landed(fin.at[t, at, pl.ds(0, (Z - (own == root)) * cw)], ro_r.at[t, h])
+                tg[t, at] = layer_norm(fin[t, at], fgain_ref[...]).astype(BF16)
+                tbuf[t, c, 0, at] = tg[t, at, own * block:(own + 1) * block]
+
+            pl.when(s == own)(rows)
+            for to in range(S):
+                if to != own:
+                    def build(to=to, at=at, h=h):
+                        return remote(tg.at[t, at, to * block:(to + 1) * block],
+                                      tbuf.at[t, c, 0, at], tg_s.at[t], tg_r.at[t, h],
+                                      (jnp.int32(to), c, z))
+                    go(s == own, build)
         owe(s == own, tg.at[t, :, pl.ds(0, (S - 1) * block)], tg_s.at[t])
 
     def nothing():
@@ -503,8 +522,10 @@
                 relay(0)
                 if Z > 2:
                     hand_rows(Z - 1)
+                spread(t, others)
             pl.when(active)(functools.partial(project, t))
         send_state(t, active)
+        retire(t)
         if t == 0:
             load_rows.wait()
         elif t == 1:
@@ -514,7 +535,6 @@
     spread(T - 1, last)
     for before in range(1, T - 1):
         spread(before, last)
-    spread(T - 1, others)
     student()
     for before in range(1, T - 1):
         relay(before)
@@ -550,9 +570,10 @@
         sw, block = w_head.shape[1:]
         cw, fw = model // Z, sw // Z
         grain = tokens // 8
-        straight, turns = 5 * grain, 3
-        pieces = ((0, 2 * grain), (2 * grain, 2 * grain), (4 * grain, grain), (straight, 3 * grain))
+        straight, turns = 6 * grain, 2
+        pieces = ((0, 2 * grain), (2 * grain, 2 * grain), (4 * grain, 2 * grain), (straight, 2 * grain))
         R = len(pieces)
+        cuts = 2 if share % 32 == 0 else 1
         vmem = pl.BlockSpec(memory_space=pltpu.VMEM)
         hbm = pl.BlockSpec(memory_space=pl.ANY)
         dma = pltpu.SemaphoreType.DMA
@@ -561,7 +582,7 @@
             functools.partial(window_kernel, S, M, Z, T, pieces, turns),
             out_shape=(
                 jax.ShapeDtypeStruct((share, model), BF16),
-                jax.ShapeDtypeStruct((fw, block), F32),
+                jax.ShapeDtypeStruct((fw, block), BF16),
             ),
             in_specs=[hbm, vmem, vmem, hbm, hbm, vmem, hbm, vmem, hbm],
             out_specs=(hbm, hbm),
@@ -585,17 +606,18 @@
                 pltpu.VMEM((tokens, model), BF16),
                 pltpu.VMEM((fw, block), F32),
                 pltpu.VMEM((T - 1, tokens - straight, model), BF16),
+                pltpu.VMEM((fw, block), BF16),
                 dma((5,)), dma((4,)), dma((4 if block % 512 == 0 else 1,)),
                 dma((1,)), dma((K,)), dma((1,)), dma((K,)),
                 dma((T,)), dma((T,)),
                 dma((T - 1, 2)), dma((T - 1, R)),
                 dma((T - 1, K, 2)), dma((T - 1, K, R)),
                 dma((T - 1, K, 2)), dma((T - 1, K, R)),
-                dma((T,)), dma((T,)),
+                dma((T,)), dma((T, cuts)),
                 dma((1,)), dma((1,)),
-                dma((T,)), dma((T,)),
+                dma((T,)), dma((T, cuts)),
                 dma((K, 2)), dma((K,)), dma((K, S - 1)), dma((K,)),
-                dma((T,)), dma((T, K)),
+                dma((T,)), dma((T, K, cuts)),
                 dma((T,)), dma((T, max(M - 1, 1))),
                 dma((T - 1,)), dma((T - 1, turns)), dma((T - 1,)), dma((T - 1, turns)),
             ],
@@ -606,7 +628,7 @@
             in_flight[0, 0], segments, norm_gain, jnp.transpose(w_qkv[0], (1, 0, 2)), w_out[0],
             final_gain[None], student_rows[0], student_gain, w_head[0],
         )
-        return adv[None, None], grad[None]
+        return adv[None, None], grad[None].astype(F32)
 
     in_specs = (
         P("section", "student", None, None),

time: 123 us -> 121 us (0.984); the launches traced: 120 us -> 120 us
  local copies, waits for them, and re-layouts: 3.98 us -> 1.67 us
  other arithmetic: 0 us -> 2.13 us
    unnamed x2 -> x1, local copies, waits for them, and re-layouts: 3.98 us -> 1.67 us
    convert_element_type x0 -> x1, other arithmetic: none -> 2.13 us  [on_device(): return (adv[None, None], grad[None].astype(F32))]
where the time goes in v4:
time: 121 us; the launch traced here: 120 us
  Pallas kernels  115 us (95%)
  other arithmetic  2.13 us (2%)
  local copies, waits for them, and re-layouts  1.67 us (1%)
    pallas_call x1, Pallas kernels, on_device(): pl.pallas_call(functools.partial(window_kernel, S, M, Z, T, pieces, turns...  115 us

profile of v4, /device:TPU:1, one launch (start us, length us, event | category | flops | bytes accessed | tf_op | source)
XLA Modules:
  0.0 119.8 jit_solution(1218408487463519228)
XLA Ops:
  0.6 115.4 %shard_map.104 = (bf16[32,4096]{1,0:T(8,128)(2,1)}, bf16[256,1024]{1,0:T(8,128)(2,1)}) custom-call(bf16[128,4096]{1,0:T(8,128)(2,1)} %bitcast.15, s32[4,1,128]{2,1,0:T(1,128)} %seg_ref.1, f32[1,4096]{1,0:T(1,128)} %gain_ref.1, bf16[3,4096,256]{2,1,0:T(8,128)(2,1)} %bitcast.12, bf16[256,4096]{1,0:T(8,128)(2,1)} %bitcast.13, f32[1,4096]{1,0:T(1,128)} %bitcast.18, ...), custom_call_target="tpu_custom_call" | custom-call | tf_op jit(solution)/shard_map/pallas_call | solution.py:581
  116.0 2.1 %bitcast_convert_fusion = f32[1,256,1024]{2,1,0:T(8,128)} fusion(bf16[256,1024]{1,0:T(8,128)(2,1)} %get-tuple-element.5), kind=kLoop, calls=%fused_computation | loop fusion | flops 262144 | bytes 1572864 | tf_op jit(solution)/shard_map/convert_element_type | solution.py:631
  118.2 1.7 %copy.12 = bf16[1,1,32,4096]{3,2,1,0:T(8,128)(2,1)} copy(bf16[1,1,32,4096]{3,2,1,0:T(8,128)(2,1)} %bitcast.17) | data formatting | bytes 524288
